TPU v7x, 32 devices: a whole 2x2x4 slice. The times are simulated.
32 devices in a mesh: rows: 4 (over x, core), feat: 8 (over z, y).
Axes of the slice: x: 2, y: 2, z: 4, core: 2. Of those that a mesh axis runs over, the one named last changes fastest.
Arguments:
- embeddings: bfloat16 [512, 1024], P(('rows', 'feat')), may hold values from -12 to 12
- freqs: bfloat16 [1024, 65536], P(None, 'feat'), may hold values from -0.1875 to 0.1875
- phases: float32 [65536], P('feat'), may hold values from 0 to 6.2831855
- sketch: bfloat16 [65536, 256], P('feat'), may hold values from -0.0234375 to 0.0234375
Outputs:
- basis: float32 [512, 256], P(('rows', 'feat'))
- coeffs: float32 [256, 65536], P(None, 'feat')
All inputs are finite; a program needn't handle non-finite values.
Results may differ from a plain program's by a relative error of at most 0.0048.
Values may be sent and summed in bfloat16 or wider, within the bound.
A program may use at most 128 MiB of HBM per device.

v0:
```python
import jax
import jax.numpy as jnp
from jax import lax
from jax.sharding import PartitionSpec as P


def per_device(embeddings, freqs, phases, sketch):
    rows_dev = embeddings.shape[0]
    row_count = rows_dev * lax.axis_size("feat") * lax.axis_size("rows")
    mixed = jnp.dot(
        lax.all_gather(embeddings, "feat", axis=0, tiled=True),
        freqs,
        preferred_element_type=jnp.float32,
    )
    features = jnp.cos(mixed + phases).astype(jnp.bfloat16)
    owned_rows = lax.psum_scatter(
        jnp.dot(features, sketch, preferred_element_type=jnp.float32),
        "feat",
        scatter_dimension=0,
        tiled=True,
    )
    local_gram = jnp.dot(owned_rows.T, owned_rows, precision=lax.Precision.HIGHEST)
    gram_matrix = lax.psum(local_gram, ("rows", "feat")) / row_count
    factor = jnp.linalg.cholesky(gram_matrix)
    basis = jax.scipy.linalg.solve_triangular(factor, owned_rows.T, lower=True).T
    block_basis = lax.all_gather(basis.astype(jnp.bfloat16), "feat", axis=0, tiled=True)
    partial_value = lax.dot_general(
        block_basis, features, (((0,), (0,)), ((), ())), preferred_element_type=jnp.float32
    )
    coeffs = lax.psum(partial_value, "rows") / row_count
    return (basis, coeffs)


def solution(mesh):
    placed = (P(("rows", "feat"), None), P(None, "feat"), P("feat"), P("feat", None))
    return jax.shard_map(
        per_device,
        mesh=mesh,
        in_specs=placed,
        out_specs=(P(("rows", "feat"), None), P(None, "feat")),
        check_vma=False,
    )
```

profile of v0, /device:TPU:0, one launch (start us, length us, event | category | flops | bytes accessed | tf_op | source)
XLA Modules:
  0.0 516.5 jit_solution(3243274491165157878)
XLA Ops:
  7.2 0.0 reduce-scatter.2.cloned.1.call-start
  7.2 32.7 %all_gather.6 = bf16[128,1024]{1,0:T(8,128)(2,1)S(1)} all-gather(bf16[16,1024]{1,0:T(8,128)(2,1)} %param.4), channel_id=1, replica_groups=mesh['rows'=4,'feat'=8] {'feat'}, dimensions={0}, use_global_device_ids=true | all-gather | bytes 294912 | tf_op jit(solution)/shard_map/all_gather | solution.py:11
  39.9 0.0 copy-start
  40.0 18.1 %fusion.1 = bf16[128,8192]{1,0:T(8,128)(2,1)S(1)} fusion(bf16[128,1024]{1,0:T(8,128)(2,1)S(1)} %all_gather.6, bf16[1024,8192]{1,0:T(8,128)(2,1)} %param.5, f32[8192]{0:T(1024)} %param.6), kind=kOutput, calls=%fused_computation.4 | convolution fusion | flops 2149580800 | bytes 19169280 | tf_op jit(solution)/shard_map/dot_general | solution.py:10
  58.1 0.0 copy-done
  58.1 1.5 fusion.12
  59.6 0.0 reduce-scatter.2.cloned.1.call-update
  59.6 0.0 all-reduce.4.cloned.1.call-start
  59.6 62.0 %reduce-scatter.2.cloned.1.call-done = f32[16,256]{1,0:T(8,128)} async-done(((f32[128,256]{1,0:T(8,128)}), f32[16,256]{1,0:T(8,128)}) %reduce-scatter.2.cloned.1.call-update) | async-done | bytes 16400 | tf_op jit(solution)/shard_map/reduce_scatter | solution.py:16
  121.6 0.0 copy-start.1
  121.6 1.9 fusion.13
  123.6 0.0 all-reduce.4.cloned.1.call-update
  123.6 0.2 all-reduce.6.cloned.1.call-start
  123.8 128.0 %all-reduce.4.cloned.1.call-done = f32[256,256]{0,1:T(8,128)} async-done(((f32[256,256]{0,1:T(8,128)}), f32[256,256]{0,1:T(8,128)}) %all-reduce.4.cloned.1.call-update) | async-done | bytes 262160 | tf_op jit(solution)/shard_map/psum | solution.py:23
  251.8 1.0 broadcast_multiply_fusion.1
  252.8 0.1 copy.7
  252.9 1.0 fusion.2
  253.9 11.7 %cholesky.50 = f32[128,128]{1,0:T(8,128)S(1)} custom-call(f32[128,128]{1,0:T(8,128)S(1)} %cholesky.118), custom_call_target="Cholesky" | custom-call | tf_op jit(solution)/shard_map/jit(cholesky)/cholesky | solution.py:24
  265.7 9.8 %custom-call.15 = f32[1,128,128]{1,2,0:T(8,128)S(1)} custom-call(f32[1,128,128]{2,1,0:T(8,128)S(1)} %get-tuple-element.25), custom_call_target="InvertDiagBlocksLowerTriangular" | custom-call | tf_op jit(solution)/shard_map/jit(cholesky)/cholesky | solution.py:24
  275.5 0.2 constant_dynamic-update-slice_fusion.1
  275.7 0.3 convolution_subtract_fusion
  276.0 11.7 %cholesky.105 = f32[128,128]{1,0:T(8,128)S(1)} custom-call(f32[128,128]{1,0:T(8,128)S(1)} %convolution_subtract_fusion), custom_call_target="Cholesky" | custom-call | tf_op jit(solution)/shard_map/jit(cholesky)/cholesky | solution.py:24
  287.8 0.7 compare_reduce_fusion
  289.9 0.1 triangular_solve.57
  289.9 4.3 while.1
  290.1 0.6 fusion.28
  290.7 1.4 bitcast_dynamic-update-slice_fusion.2
  292.2 0.6 fusion.28
  292.8 1.4 bitcast_dynamic-update-slice_fusion.2
  294.2 19.7 %custom-call.16 = f32[2,128,128]{1,2,0:T(8,128)S(1)} custom-call(f32[2,128,128]{2,1,0:T(8,128)S(1)} %get-tuple-element.9), custom_call_target="InvertDiagBlocksLowerTriangular" | custom-call | tf_op jit(solution)/shard_map/jit(_solve_triangular)/triangular_solve | solution.py:25
  313.9 0.0 copy-done.1
  313.9 0.2 fusion.5
  314.1 0.2 convolution_subtract_fusion.1
  314.3 0.2 fusion.4
  314.5 0.6 fusion.10
  315.1 30.5 %all_gather.7 = bf16[128,256]{1,0:T(8,128)(2,1)S(1)} all-gather(bf16[16,256]{1,0:T(8,128)(2,1)S(1)} %get-tuple-element.18), channel_id=1, replica_groups=mesh['rows'=4,'feat'=8] {'feat'}, dimensions={0}, use_global_device_ids=true | all-gather | bytes 73728 | tf_op jit(solution)/shard_map/all_gather | solution.py:26
  345.6 4.7 fusion.14
  350.3 0.0 all-reduce.6.cloned.1.call-update
  350.3 152.0 %all-reduce.6.cloned.1.call-done = f32[256,8192]{1,0:T(8,128)} async-done(((f32[256,8192]{1,0:T(8,128)}), f32[256,8192]{1,0:T(8,128)}) %all-reduce.6.cloned.1.call-update) | async-done | bytes 8388624 | tf_op jit(solution)/shard_map/psum | solution.py:30
  502.3 7.7 %broadcast_multiply_fusion = f32[256,8192]{1,0:T(8,128)} fusion(f32[256,8192]{1,0:T(8,128)} %all-reduce.6.cloned.1.call-done), kind=kLoop, calls=%fused_computation.5 | loop fusion | flops 2097152 | bytes 16777216 | tf_op jit(solution)/shard_map/div | solution.py:30
  (9 shorter events, 0.1 us)
Async XLA Ops:
  7.2 114.5 %reduce-scatter.2.cloned.1.call-start = ((), (), s32[]{:S(2)}) async-start(), calls=%async_computation.1 | async-start | bytes 147456 | tf_op jit(solution)/shard_map/reduce_scatter | solution.py:16
  39.9 18.2 %copy-start = (bf16[8192,256]{1,0:T(8,128)(2,1)S(1)}, bf16[8192,256]{1,0:T(8,128)(2,1)}, u32[]{:S(2)}) copy-start(bf16[8192,256]{1,0:T(8,128)(2,1)} %param.7) | copy-start | bytes 12582916
  59.6 192.2 %all-reduce.4.cloned.1.call-start = ((), (), s32[]{:S(2)}) async-start(), calls=%async_computation.2 | async-start | bytes 524288 | tf_op jit(solution)/shard_map/psum | solution.py:23
  121.6 192.3 %copy-start.1 = (f32[16,256]{1,0:T(8,128)S(1)}, f32[16,256]{1,0:T(8,128)}, u32[]{:S(2)}) copy-start(f32[16,256]{1,0:T(8,128)} %reduce-scatter.2.cloned.1.call-done) | copy-start | bytes 49156
  123.6 378.7 %all-reduce.6.cloned.1.call-start = ((), (), s32[]{:S(2)}) async-start(), calls=%async_computation.3 | async-start | bytes 16777216 | tf_op jit(solution)/shard_map/psum | solution.py:30
Sparse Core Ops, SparseCore 0:
  59.7 61.8 reduce-scatter.1
  127.7 124.0 all-reduce.3
  350.4 151.8 all-reduce.5
where the time goes:
time: 517 us
  waiting for transfers between devices  342 us (66%)
  other arithmetic  64 us (12%)
  blocking collectives  63.2 us (12%)
  matrix products  27.2 us (5%)
  between operations  15.2 us (3%)
    psum x1, waiting for transfers between devices, per_device(): coeffs = lax.psum(partial_value, 'rows') / row_count  152 us
    psum x1, waiting for transfers between devices, per_device(): gram_matrix = lax.psum(local_gram, ('rows', 'feat')) / row_count  128 us
    reduce_scatter x1, waiting for transfers between devices, per_device(): lax.psum_scatter(jnp.dot(features, sketch, preferred_element_type=jnp.flo...  62 us
    another operation x6, other arithmetic, per_device(): factor = jnp.linalg.cholesky(gram_matrix)  34 us
    all_gather x1, blocking collectives, per_device(): lax.all_gather(embeddings, 'feat', axis=0, tiled=True)  32.7 us
    all_gather x1, blocking collectives, per_device(): lax.all_gather(basis.astype(jnp.bfloat16), 'feat', axis=0, tiled=True)  30.5 us
    another operation x3, other arithmetic, per_device(): jax.scipy.linalg.solve_triangular(factor, owned_rows.T, lower=True)  19.7 us
    dot_general x1, matrix products, per_device(): jnp.dot(lax.all_gather(embeddings, 'feat', axis=0, tiled=True), freqs, pr...  18.1 us
  transfers between devices with their start and end apart: 3, of which 3 were waited for; matrix products, arithmetic and copies ran while one was open for 0% of the time, Pallas kernels for 0%

commit v1 on v0

--- a/solution.py
+++ b/solution.py
@@ -27,7 +27,7 @@
     partial_value = lax.dot_general(
         block_basis, features, (((0,), (0,)), ((), ())), preferred_element_type=jnp.float32
     )
-    coeffs = lax.psum(partial_value, "rows") / row_count
+    coeffs = jnp.sum(lax.all_gather(partial_value, "rows"), axis=0) / row_count
     return (basis, coeffs)
 
 

time: 517 us -> 581 us (1.12)
  waiting for transfers between devices: 342 us -> 391 us
  other arithmetic: 64 us -> 79.9 us
    all_gather x0 -> x1, waiting for transfers between devices: none -> 201 us  [per_device(): coeffs = jnp.sum(lax.all_gather(partial_value, 'rows'), axis=0) / row_count]
    psum x1 -> x0, waiting for transfers between devices: 152 us -> none  [per_device(): coeffs = lax.psum(partial_value, 'rows') / row_count]
    reduce_sum x0 -> x1, other arithmetic: none -> 15.9 us  [per_device(): coeffs = jnp.sum(lax.all_gather(partial_value, 'rows'), axis=0) / row_count]
where the time goes in v1:
time: 581 us
  waiting for transfers between devices  391 us (67%)
  other arithmetic  79.9 us (14%)
  blocking collectives  63.2 us (11%)
  matrix products  27.2 us (5%)
  between operations  15.2 us (3%)
    all_gather x1, waiting for transfers between devices, per_device(): coeffs = jnp.sum(lax.all_gather(partial_value, 'rows'), axis=0) / row_count  201 us
    psum x1, waiting for transfers between devices, per_device(): gram_matrix = lax.psum(local_gram, ('rows', 'feat')) / row_count  128 us
    reduce_scatter x1, waiting for transfers between devices, per_device(): lax.psum_scatter(jnp.dot(features, sketch, preferred_element_type=jnp.flo...  62 us
    another operation x6, other arithmetic, per_device(): factor = jnp.linalg.cholesky(gram_matrix)  34 us
    all_gather x1, blocking collectives, per_device(): lax.all_gather(embeddings, 'feat', axis=0, tiled=True)  32.7 us
    all_gather x1, blocking collectives, per_device(): lax.all_gather(basis.astype(jnp.bfloat16), 'feat', axis=0, tiled=True)  30.5 us
    another operation x3, other arithmetic, per_device(): jax.scipy.linalg.solve_triangular(factor, owned_rows.T, lower=True)  19.7 us
    dot_general x1, matrix products, per_device(): jnp.dot(lax.all_gather(embeddings, 'feat', axis=0, tiled=True), freqs, pr...  18.1 us
  transfers between devices with their start and end apart: 3, of which 3 were waited for; matrix products, arithmetic and copies ran while one was open for 0% of the time, Pallas kernels for 0%

profile of v1, /device:TPU:0, one launch (start us, length us, event | category | flops | bytes accessed | tf_op | source)
XLA Modules:
  0.0 581.1 jit_solution(59395947410067255)
XLA Ops:
  7.2 0.0 reduce-scatter.2.cloned.1.call-start
  7.2 32.7 %all_gather.12 = bf16[128,1024]{1,0:T(8,128)(2,1)S(1)} all-gather(bf16[16,1024]{1,0:T(8,128)(2,1)} %param.4), channel_id=1, replica_groups=mesh['rows'=4,'feat'=8] {'feat'}, dimensions={0}, use_global_device_ids=true | all-gather | bytes 294912 | tf_op jit(solution)/shard_map/all_gather | solution.py:11
  39.9 0.0 copy-start
  40.0 18.1 %fusion.1 = bf16[128,8192]{1,0:T(8,128)(2,1)S(1)} fusion(bf16[128,1024]{1,0:T(8,128)(2,1)S(1)} %all_gather.12, bf16[1024,8192]{1,0:T(8,128)(2,1)} %param.5, f32[8192]{0:T(1024)} %param.6), kind=kOutput, calls=%fused_computation.4 | convolution fusion | flops 2149580800 | bytes 19169280 | tf_op jit(solution)/shard_map/dot_general | solution.py:10
  58.1 0.0 copy-done
  58.1 1.5 fusion.12
  59.6 0.0 reduce-scatter.2.cloned.1.call-update
  59.6 0.0 all-reduce.3.cloned.1.call-start
  59.6 62.0 %reduce-scatter.2.cloned.1.call-done = f32[16,256]{1,0:T(8,128)} async-done(((f32[128,256]{1,0:T(8,128)}), f32[16,256]{1,0:T(8,128)}) %reduce-scatter.2.cloned.1.call-update) | async-done | bytes 16400 | tf_op jit(solution)/shard_map/reduce_scatter | solution.py:16
  121.6 0.0 copy-start.1
  121.6 1.9 fusion.13
  123.6 0.0 all-reduce.3.cloned.1.call-update
  123.6 0.2 all-gather.3.cloned.1.call-start
  123.8 128.0 %all-reduce.3.cloned.1.call-done = f32[256,256]{0,1:T(8,128)} async-done(((f32[256,256]{0,1:T(8,128)}), f32[256,256]{0,1:T(8,128)}) %all-reduce.3.cloned.1.call-update) | async-done | bytes 262160 | tf_op jit(solution)/shard_map/psum | solution.py:23
  251.8 1.0 broadcast_multiply_fusion.1
  252.8 0.1 copy.7
  252.9 1.0 fusion.2
  253.9 11.7 %cholesky.50 = f32[128,128]{1,0:T(8,128)S(1)} custom-call(f32[128,128]{1,0:T(8,128)S(1)} %cholesky.118), custom_call_target="Cholesky" | custom-call | tf_op jit(solution)/shard_map/jit(cholesky)/cholesky | solution.py:24
  265.7 9.8 %custom-call.15 = f32[1,128,128]{1,2,0:T(8,128)S(1)} custom-call(f32[1,128,128]{2,1,0:T(8,128)S(1)} %get-tuple-element.25), custom_call_target="InvertDiagBlocksLowerTriangular" | custom-call | tf_op jit(solution)/shard_map/jit(cholesky)/cholesky | solution.py:24
  275.5 0.2 constant_dynamic-update-slice_fusion.1
  275.7 0.3 convolution_subtract_fusion
  276.0 11.7 %cholesky.105 = f32[128,128]{1,0:T(8,128)S(1)} custom-call(f32[128,128]{1,0:T(8,128)S(1)} %convolution_subtract_fusion), custom_call_target="Cholesky" | custom-call | tf_op jit(solution)/shard_map/jit(cholesky)/cholesky | solution.py:24
  287.8 0.7 compare_reduce_fusion
  289.9 0.1 triangular_solve.57
  289.9 4.3 while.1
  290.1 0.6 fusion.28
  290.7 1.4 bitcast_dynamic-update-slice_fusion.2
  292.2 0.6 fusion.28
  292.8 1.4 bitcast_dynamic-update-slice_fusion.2
  294.2 19.7 %custom-call.16 = f32[2,128,128]{1,2,0:T(8,128)S(1)} custom-call(f32[2,128,128]{2,1,0:T(8,128)S(1)} %get-tuple-element.9), custom_call_target="InvertDiagBlocksLowerTriangular" | custom-call | tf_op jit(solution)/shard_map/jit(_solve_triangular)/triangular_solve | solution.py:25
  313.9 0.0 copy-done.1
  313.9 0.2 fusion.5
  314.1 0.2 convolution_subtract_fusion.1
  314.3 0.2 fusion.4
  314.5 0.6 fusion.10
  315.1 30.5 %all_gather.13 = bf16[128,256]{1,0:T(8,128)(2,1)S(1)} all-gather(bf16[16,256]{1,0:T(8,128)(2,1)S(1)} %get-tuple-element.18), channel_id=1, replica_groups=mesh['rows'=4,'feat'=8] {'feat'}, dimensions={0}, use_global_device_ids=true | all-gather | bytes 73728 | tf_op jit(solution)/shard_map/all_gather | solution.py:26
  345.6 4.7 fusion.14
  350.3 0.0 all-gather.3.cloned.1.call-update
  350.3 200.7 %all-gather.3.cloned.1.call-done = f32[1024,8192]{1,0:T(8,128)} async-done(((f32[256,8192]{1,0:T(8,128)}), f32[1024,8192]{1,0:T(8,128)}) %all-gather.3.cloned.1.call-update) | async-done | bytes 33554448 | tf_op jit(solution)/shard_map/all_gather | solution.py:30
  551.0 15.9 %reduce_sum.9 = f32[256,8192]{1,0:T(8,128)} reduce(f32[4,256,8192]{2,1,0:T(8,128)} %bitcast.44, f32[]{:T(128)} %constant.81.clone.1), dimensions={0}, to_apply=%region_6.7 | reduce | flops 6291456 | bytes 41943044 | tf_op jit(solution)/shard_map/reduce_sum | solution.py:30
  566.8 7.7 %broadcast_multiply_fusion = f32[256,8192]{1,0:T(8,128)} fusion(f32[256,8192]{1,0:T(8,128)} %reduce_sum.9), kind=kLoop, calls=%fused_computation.5 | loop fusion | flops 2097152 | bytes 16777216 | tf_op jit(solution)/shard_map/div | solution.py:30
  (9 shorter events, 0.1 us)
Async XLA Ops:
  7.2 114.5 %reduce-scatter.2.cloned.1.call-start = ((), (), s32[]{:S(2)}) async-start(), calls=%async_computation.1 | async-start | bytes 147456 | tf_op jit(solution)/shard_map/reduce_scatter | solution.py:16
  39.9 18.2 %copy-start = (bf16[8192,256]{1,0:T(8,128)(2,1)S(1)}, bf16[8192,256]{1,0:T(8,128)(2,1)}, u32[]{:S(2)}) copy-start(bf16[8192,256]{1,0:T(8,128)(2,1)} %param.7) | copy-start | bytes 12582916
  59.6 192.2 %all-reduce.3.cloned.1.call-start = ((), (), s32[]{:S(2)}) async-start(), calls=%async_computation.2 | async-start | bytes 524288 | tf_op jit(solution)/shard_map/psum | solution.py:23
  121.6 192.3 %copy-start.1 = (f32[16,256]{1,0:T(8,128)S(1)}, f32[16,256]{1,0:T(8,128)}, u32[]{:S(2)}) copy-start(f32[16,256]{1,0:T(8,128)} %reduce-scatter.2.cloned.1.call-done) | copy-start | bytes 49156
  123.6 427.4 %all-gather.3.cloned.1.call-start = ((), (), s32[]{:S(2)}) async-start(), calls=%async_computation.3 | async-start | bytes 41943040 | tf_op jit(solution)/shard_map/all_gather | solution.py:30
Sparse Core Ops, SparseCore 0:
  59.7 61.8 reduce-scatter.1
  127.7 124.0 all-reduce.2
  350.4 200.5 all-gather.2
